TPU v7x, 512 devices: a whole 4x8x8 slice. The times are simulated.
512 devices in a mesh: band: 32 (over x, y_lo, core), grid: 16 (over z, y_hi).
Axes of the slice: x: 4, y: 8 (y_hi: 2, y_lo: 4; y = y_hi * 4 + y_lo), z: 8, core: 2. Of those that a mesh axis runs over, the one named last changes fastest.
Arguments:
- orbitals: bfloat16 [64, 160, 25600], P('band', 'grid'), may hold values from -6 to 6
- source_index: int32 [2], replicated, may hold values from 0 to 63
Outputs:
- fock_exchange: bfloat16 [64, 160, 25600], P('band', 'grid')
All inputs are finite; a program needn't handle non-finite values.
Results may differ from a plain program's by a relative error of at most 0.012.
The roundings to bfloat16 on the way count: a program that leaves them out, or rounds other values in their place, can miss the bound.
Values may be sent and summed in bfloat16 or wider, within the bound.
A program may use at most 64 MiB of HBM per device.

v0:
```python
import math
import jax
import jax.numpy as jnp
from jax import lax
from jax.sharding import PartitionSpec as P

spacing = 0.3


def broadcast(x, axis, root):
    mine = lax.axis_index(axis) == root
    return lax.psum(jnp.where(mine, x, jnp.zeros_like(x)), axis)


def cas_table(extent):
    wavenum = jnp.arange(extent, dtype=jnp.int32)
    products_mod = wavenum[:, None] * wavenum[None, :] % extent
    radians = products_mod.astype(jnp.float32) * (2.0 * math.pi / extent)
    return ((jnp.cos(radians) + jnp.sin(radians)) / math.sqrt(extent)).astype(jnp.bfloat16)


def wave_square(indices, extent):
    folded = jnp.minimum(indices, extent - indices).astype(jnp.float32)
    return folded * folded


def transform(grid_data, cas_matrix, pattern):
    return jnp.einsum(pattern, grid_data, cas_matrix, preferred_element_type=jnp.float32)


def potentials(pair_rho, cas_matrix, kernel_block):
    along_z = transform(pair_rho, cas_matrix, "pxyz,kz->pxyk").astype(jnp.bfloat16)
    along_y = transform(along_z, cas_matrix, "pxyz,ky->pxkz").astype(jnp.bfloat16)
    scaled = (
        kernel_block
        * transform(
            lax.all_to_all(along_y, "grid", split_axis=2, concat_axis=1, tiled=True),
            cas_matrix,
            "pxyz,kx->pkyz",
        )
    ).astype(jnp.bfloat16)
    back_x = transform(scaled, cas_matrix, "pxyz,kx->pkyz").astype(jnp.bfloat16)
    returned = lax.all_to_all(back_x, "grid", split_axis=1, concat_axis=2, tiled=True)
    again_y = transform(returned, cas_matrix, "pxyz,ky->pxkz").astype(jnp.bfloat16)
    return transform(again_y, cas_matrix, "pxyz,kz->pxyk")


def fetch_source(orbitals, which):
    local_count = orbitals.shape[0]
    local_slab = lax.dynamic_index_in_dim(orbitals, which % local_count, 0, keepdims=False)
    return broadcast(local_slab, "band", which // local_count)


def shards(orbitals, source_index):
    local_count = orbitals.shape[0]
    planes = orbitals.shape[1]
    extent = planes * lax.axis_size("grid")
    orbitals = orbitals.reshape(local_count, planes, extent, extent)
    source_count = source_index.shape[0]
    cas_matrix = cas_table(extent)
    columns = extent // lax.axis_size("grid")
    offset = lax.axis_index("grid") * columns
    square_x = wave_square(jnp.arange(extent, dtype=jnp.int32), extent)
    square_y = wave_square(offset + jnp.arange(columns, dtype=jnp.int32), extent)
    total_sq = square_x[:, None, None] + square_y[None, :, None] + square_x[None, None, :]
    strength = (extent * spacing) ** 2 / math.pi
    kernel_block = jnp.where(total_sq > 0, strength / (total_sq + 1.0), 0.0)
    fetched = None
    fetched = [fetch_source(orbitals, source_index[number]) for number in range(source_count)]
    stacked = jnp.stack(fetched)[:, None].astype(jnp.float32)
    pair_rho = (stacked * orbitals[None].astype(jnp.float32)).astype(jnp.bfloat16)
    pair_rho = pair_rho.reshape(source_count * local_count, planes, extent, extent)
    potential = potentials(pair_rho, cas_matrix, kernel_block)
    potential = potential.reshape(source_count, local_count, planes, extent, extent)
    summed_total = jnp.sum(stacked * potential, axis=0)
    result = (-summed_total).astype(jnp.bfloat16)
    return result.reshape(local_count, planes, extent * extent)


def solution(mesh):
    return jax.shard_map(
        shards,
        mesh=mesh,
        in_specs=(P("band", "grid", None), P()),
        out_specs=P("band", "grid", None),
        check_vma=False,
    )
```

profile of v0, /device:TPU:54, one launch (start us, length us, event | category | flops | bytes accessed | tf_op | source)
XLA Modules:
  0.0 598.6 jit_solution(17245803974825692510)
XLA Ops:
  6.5 0.0 all-reduce.3.cloned.1.call-start
  6.5 1.3 fusion.89
  13.0 3.7 reshape.107
  16.7 1.3 dynamic-slice_select_fusion.1
  18.0 0.0 all-reduce.3.cloned.1.call-update
  18.0 281.7 %all-reduce.3.cloned.1.call-done = (bf16[1,10,160,160]{3,2,0,1:T(8,128)(2,1)}, bf16[1,10,160,160]{3,2,0,1:T(8,128)(2,1)}) async-done(((bf16[1,10,160,160]{3,2,0,1:T(8,128)(2,1)}, bf16[1,10,160,160]{3,2,0,1:T(8,128)(2,1)}), (bf16[1,10,160,160]{3,2,0,1:T(8,128)(2,1)}, bf16[1,10,160,160]{3,2,0,1:T(8,128)(2,1)})) %all-reduce.3.cloned.1.call-update) | async-done | bytes 1024016 | tf_op jit(solution)/shard_map/psum | solution.py:12
  299.7 5.3 multiply_convert_fusion.1
  305.0 4.6 convert_bitcast_fusion.1
  309.6 4.2 copy.35
  313.8 12.8 %all-to-all-start = ((bf16[4,10,160,160]{3,0,1,2:T(4,128)(2,1)}), bf16[4,10,160,160]{3,0,1,2:T(4,128)(2,1)S(1)}, u32[]{:S(2)}, u32[]{:S(2)}) async-start(bf16[4,10,160,160]{3,0,1,2:T(4,128)(2,1)} %copy.35), calls=%async_computation | async-start | bytes 6553600 | tf_op jit(solution)/shard_map/all_to_all | solution.py:37
  326.6 0.1 broadcast_add_fusion
  326.7 1.6 fusion.30
  328.2 145.4 %all-to-all-done = bf16[4,10,160,160]{3,0,1,2:T(4,128)(2,1)S(1)} async-done(((bf16[4,10,160,160]{3,0,1,2:T(4,128)(2,1)}), bf16[4,10,160,160]{3,0,1,2:T(4,128)(2,1)S(1)}, u32[]{:S(2)}, u32[]{:S(2)}) %all-to-all-start) | async-done | bytes 2048032 | tf_op jit(solution)/shard_map/all_to_all | solution.py:37
  473.7 2.8 copy.37
  476.5 5.9 convert_bitcast_fusion
  482.3 2.5 copy.39
  484.9 90.1 %all_to_all.36 = bf16[4,160,10,160]{3,0,2,1:T(4,128)(2,1)S(1)} all-to-all(bf16[4,160,10,160]{3,0,2,1:T(4,128)(2,1)S(1)} %copy.39), channel_id=1, replica_groups=mesh['band'=32,'grid'=16] {'grid'}, dimensions={1} | all-to-all | bytes 4096000 | tf_op jit(solution)/shard_map/all_to_all | solution.py:43
  574.9 1.3 copy.40
  576.3 5.3 fusion.3
  581.5 5.0 multiply_reduce_fusion
  586.6 0.4 negate_convert_fusion
  587.0 2.7 reshape.112
  589.7 2.0 copy.45
  (2 shorter events, 0.0 us)
Async XLA Ops:
  6.5 293.2 %all-reduce.3.cloned.1.call-start = ((), (), s32[]{:S(2)}) async-start(), calls=%async_computation.2 | async-start | bytes 3276800 | tf_op jit(solution)/shard_map/psum | solution.py:12
  313.8 159.9 %all-to-all-start = ((bf16[4,10,160,160]{3,0,1,2:T(4,128)(2,1)}), bf16[4,10,160,160]{3,0,1,2:T(4,128)(2,1)S(1)}, u32[]{:S(2)}, u32[]{:S(2)}) async-start(bf16[4,10,160,160]{3,0,1,2:T(4,128)(2,1)} %copy.35), calls=%async_computation | async-start | bytes 6553600 | tf_op jit(solution)/shard_map/all_to_all | solution.py:37
Sparse Core Ops, SparseCore 0:
  18.1 281.5 all-reduce.2
where the time goes:
time: 599 us
  waiting for transfers between devices  427 us (71%)
  blocking collectives  90.1 us (15%)
  local copies, waits for them, and re-layouts  20.6 us (3%)
  between operations  18.5 us (3%)
  matrix products  15.7 us (3%)
  other arithmetic  13.7 us (2%)
  starting transfers between devices  12.8 us (2%)
    psum x1, waiting for transfers between devices, broadcast(): return lax.psum(jnp.where(mine, x, jnp.zeros_like(x)), axis)  282 us
    all_to_all x1, waiting for transfers between devices, potentials(): lax.all_to_all(along_y, 'grid', split_axis=2, concat_axis=1, tiled=True)  145 us
    all_to_all x1, blocking collectives, potentials(): lax.all_to_all(back_x, 'grid', split_axis=1, concat_axis=2, tiled=True)  90.1 us
    dot_general x3, matrix products, transform(): jnp.einsum(pattern, grid_data, cas_matrix, preferred_element_type=jnp.flo...  15.7 us
    all_to_all x1, starting transfers between devices, potentials(): lax.all_to_all(along_y, 'grid', split_axis=2, concat_axis=1, tiled=True)  12.8 us
  transfers between devices with their start and end apart: 2, of which 2 were waited for; matrix products, arithmetic and copies ran while one was open for 0% of the time, Pallas kernels for 0%

commit v1 on v0

--- a/solution.py
+++ b/solution.py
@@ -7,9 +7,15 @@
 spacing = 0.3
 
 
+def gather_and_add(x, axis):
+    parts = lax.all_gather(x, axis, axis=0, tiled=False)
+    total = parts.sum(axis=0)
+    return total
+
+
 def broadcast(x, axis, root):
     mine = lax.axis_index(axis) == root
-    return lax.psum(jnp.where(mine, x, jnp.zeros_like(x)), axis)
+    return gather_and_add(jnp.where(mine, x, jnp.zeros_like(x)), axis)
 
 
 def cas_table(extent):

time: 599 us -> 671 us (1.12)
  the two profiles are of different devices: /device:TPU:54 before, /device:TPU:50 now
where the time goes in v1:
time: 671 us; the launch traced here: 670 us
  waiting for transfers between devices  409 us (61%)
  blocking collectives  135 us (20%)
  other arithmetic  45.6 us (7%)
  local copies, waits for them, and re-layouts  28.3 us (4%)
  matrix products  21 us (3%)
  between operations  18.6 us (3%)
  starting transfers between devices  12.8 us (2%)
    all_gather x2, waiting for transfers between devices, gather_and_add(): parts = lax.all_gather(x, axis, axis=0, tiled=False)  290 us
    all_to_all x1, blocking collectives, potentials(): lax.all_to_all(back_x, 'grid', split_axis=1, concat_axis=2, tiled=True)  135 us
    all_to_all x1, waiting for transfers between devices, potentials(): lax.all_to_all(along_y, 'grid', split_axis=2, concat_axis=1, tiled=True)  118 us
    reduce_sum x2, other arithmetic, gather_and_add(): total = parts.sum(axis=0)  32 us
    dot_general x3, matrix products, transform(): jnp.einsum(pattern, grid_data, cas_matrix, preferred_element_type=jnp.flo...  21 us
  transfers between devices with their start and end apart: 3, of which 3 were waited for; matrix products, arithmetic and copies ran while one was open for 3% of the time, Pallas kernels for 0%

profile of v1, /device:TPU:50, one launch (start us, length us, event | category | flops | bytes accessed | tf_op | source)
XLA Modules:
  0.0 670.5 jit_solution(2784069435522040971)
XLA Ops:
  6.5 1.3 fusion.89
  13.0 3.7 reshape.101
  16.7 1.4 dynamic-slice_select_fusion.1
  18.2 0.7 all-gather.5.cloned.1.call-update
  18.9 153.4 %all-gather.3.cloned.1.call-done = bf16[32,10,160,160]{3,2,0,1:T(8,128)(2,1)} async-done(((bf16[1,10,160,160]{3,2,0,1:T(8,128)(2,1)}), bf16[32,10,160,160]{3,2,0,1:T(8,128)(2,1)}) %all-gather.3.cloned.1.call-update) | async-done | bytes 16384016 | tf_op jit(solution)/shard_map/all_gather | solution.py:11
  172.3 16.0 %reduce_sum.33 = bf16[10,160,160]{2,1,0:T(8,128)(2,1)} reduce(bf16[32,10,160,160]{3,2,0,1:T(8,128)(2,1)} %all-gather.3.cloned.1.call-done, bf16[]{:T(256)} %constant.72.clone.1), dimensions={0}, to_apply=%region_0.1 | reduce | flops 7936000 | bytes 16896002 | tf_op jit(solution)/shard_map/reduce_sum | solution.py:12
  188.3 137.0 %all-gather.5.cloned.1.call-done = bf16[32,10,160,160]{3,2,0,1:T(8,128)(2,1)} async-done(((bf16[1,10,160,160]{3,2,0,1:T(8,128)(2,1)}), bf16[32,10,160,160]{3,2,0,1:T(8,128)(2,1)}) %all-gather.5.cloned.1.call-update) | async-done | bytes 16384016 | tf_op jit(solution)/shard_map/all_gather | solution.py:11
  325.3 16.0 %reduce_sum.34 = bf16[10,160,160]{2,1,0:T(8,128)(2,1)} reduce(bf16[32,10,160,160]{3,2,0,1:T(8,128)(2,1)} %all-gather.5.cloned.1.call-done, bf16[]{:T(256)} %constant.72.clone.1), dimensions={0}, to_apply=%region_1.2 | reduce | flops 7936000 | bytes 16896002 | tf_op jit(solution)/shard_map/reduce_sum | solution.py:12
  341.3 1.9 maximum_convert_fusion
  343.2 3.8 multiply_convert_fusion.1
  347.0 6.3 convert_bitcast_fusion.1
  353.3 6.2 copy.30
  359.5 12.8 %all-to-all-start = ((bf16[4,10,160,160]{3,0,1,2:T(4,128)(2,1)}), bf16[4,10,160,160]{3,0,1,2:T(4,128)(2,1)}, u32[]{:S(2)}, u32[]{:S(2)}) async-start(bf16[4,10,160,160]{3,0,1,2:T(4,128)(2,1)} %copy.30), calls=%async_computation | async-start | bytes 6553600 | tf_op jit(solution)/shard_map/all_to_all | solution.py:43
  372.4 1.6 fusion.30
  373.9 118.3 %all-to-all-done = bf16[4,10,160,160]{3,0,1,2:T(4,128)(2,1)} async-done(((bf16[4,10,160,160]{3,0,1,2:T(4,128)(2,1)}), bf16[4,10,160,160]{3,0,1,2:T(4,128)(2,1)}, u32[]{:S(2)}, u32[]{:S(2)}) %all-to-all-start) | async-done | bytes 2048032 | tf_op jit(solution)/shard_map/all_to_all | solution.py:43
  492.2 4.8 copy.32
  497.0 7.5 %convert_bitcast_fusion = bf16[4,160,10,160]{3,1,2,0:T(8,128)(2,1)} fusion(f32[160,10,160]{2,0,1:T(8,128)} %fusion.30, bf16[4,160,10,160]{3,0,2,1:T(4,128)(2,1)} %bitcast.45), kind=kOutput, calls=%fused_computation.13 | convolution fusion | flops 659046400 | bytes 5120000 | tf_op jit(solution)/shard_map/pxyz,kx->pkyz/dot_general | solution.py:34
  504.5 4.5 copy.34
  509.0 134.7 %all_to_all.36 = bf16[4,160,10,160]{3,0,2,1:T(4,128)(2,1)S(1)} all-to-all(bf16[4,160,10,160]{3,0,2,1:T(4,128)(2,1)S(1)} %copy.34), channel_id=1, replica_groups=mesh['band'=32,'grid'=16] {'grid'}, dimensions={1} | all-to-all | bytes 4096000 | tf_op jit(solution)/shard_map/all_to_all | solution.py:49
  643.7 3.1 copy.35
  646.9 7.2 %fusion.3 = f32[4,10,160,160]{3,2,1,0:T(8,128)} fusion(bf16[4,10,160,160]{3,0,2,1:T(4,128)(2,1)} %bitcast.43), kind=kOutput, calls=%fused_computation.5 | convolution fusion | flops 656998400 | bytes 6144000 | tf_op jit(solution)/shard_map/pxyz,kz->pxyk/dot_general | solution.py:34
  654.1 4.4 multiply_reduce_fusion
  658.9 2.7 reshape.104
  661.6 2.0 copy.40
  (11 shorter events, 0.6 us)
Async XLA Ops:
  6.5 165.8 %all-gather.3.cloned.1.call-start = ((), (), s32[]{:S(2)}) async-start(), calls=%async_computation.2 | async-start | bytes 27033600 | tf_op jit(solution)/shard_map/all_gather | solution.py:11
  16.7 171.7 %copy-start = (bf16[2,10,160,160]{3,2,0,1:T(8,128)(2,1)}, bf16[2,10,160,160]{3,2,0,1:T(8,128)(2,1)S(1)}, u32[]{:S(2)}) copy-start(bf16[2,10,160,160]{3,2,0,1:T(8,128)(2,1)S(1)} %reshape.101) | copy-start | bytes 3072004
  18.2 307.1 %all-gather.5.cloned.1.call-start = ((), (), s32[]{:S(2)}) async-start(), calls=%async_computation.3 | async-start | bytes 27033600 | tf_op jit(solution)/shard_map/all_gather | solution.py:11
  341.3 1.9 copy-start.1
  359.5 132.7 %all-to-all-start = ((bf16[4,10,160,160]{3,0,1,2:T(4,128)(2,1)}), bf16[4,10,160,160]{3,0,1,2:T(4,128)(2,1)}, u32[]{:S(2)}, u32[]{:S(2)}) async-start(bf16[4,10,160,160]{3,0,1,2:T(4,128)(2,1)} %copy.30), calls=%async_computation | async-start | bytes 6553600 | tf_op jit(solution)/shard_map/all_to_all | solution.py:43
Sparse Core Ops, SparseCore 0:
  18.3 154.0 all-gather.2
  174.4 150.8 all-gather.4
